TPU v7x, 32 devices: a whole 2x2x4 slice. The times are simulated.
32 devices in a mesh: section: 4 (over z), dp: 2 (over x), tensor: 4 (over y, core).
Axes of the slice: x: 2, y: 2, z: 4, core: 2. Of those that a mesh axis runs over, the one named last changes fastest.
Arguments:
- sent: bfloat16 [8, 384, 6144], P('section', 'dp', 'tensor'), may hold values from -6 to 6
- stashed_inputs: bfloat16 [16, 96, 6144], P('section', 'dp', 'tensor'), may hold values from -6 to 6
- table: int32 [4, 4], P('section'), may hold values from 0 to 3, each once within a row
- embedded: bfloat16 [384, 6144], P('dp', 'tensor'), may hold values from -6 to 6
- loss_gradient: bfloat16 [384, 6144], P('dp', 'tensor'), may hold values from -6 to 6
- weight: bfloat16 [4, 6144, 6144], P('section', None, 'tensor'), may hold values from -0.078125 to 0.078125
- adapter_down_weight: bfloat16 [4, 6144, 128], P('section'), may hold values from -0.078125 to 0.078125
- adapter_up_weight: bfloat16 [4, 128, 6144], P('section', None, 'tensor'), may hold values from -0.5 to 0.5
Outputs:
- forward_output: bfloat16 [4, 384, 6144], P('section', 'dp', 'tensor')
- backward_output: bfloat16 [4, 384, 6144], P('section', 'dp', 'tensor')
- down_gradient: bfloat16 [4, 6144, 128], P('section', 'tensor')
- up_gradient: bfloat16 [4, 128, 6144], P('section', None, 'tensor')
Inputs may be any that keep to these rules, and one draw needn't show every extreme that they name: Each row of table is a permutation of 0 to 3.
All inputs are finite; a program needn't handle non-finite values.
Results may differ from a plain program's by a relative error of at most 0.019.
Values may be sent and summed in bfloat16 or wider, within the bound.
A program may use at most 64 MiB of HBM per device.

v0:
```python
import jax
import jax.numpy as jnp
from jax import lax
from jax.sharding import PartitionSpec as P

coef = 0.7978845608028654


def shifted(block, axis, distance):
    devices = range(lax.axis_size(axis))
    route = [(i - distance, i) for i in devices if i - distance in devices]
    return lax.ppermute(block, axis, route)


def gelu_pair(u):
    inner = coef * (u + 0.044715 * u * u * u)
    tanh_v = jnp.tanh(inner)
    value = 0.5 * u * (1.0 + tanh_v)
    slope = 0.5 * (1.0 + tanh_v) + 0.5 * u * (1.0 - tanh_v * tanh_v) * coef * (
        1.0 + 3.0 * 0.044715 * u * u
    )
    return (value, slope)


def on_device(
    sent,
    stashed_inputs,
    table,
    embedded,
    loss_gradient,
    weight,
    adapter_down_weight,
    adapter_up_weight,
):
    section = lax.axis_index("section")
    sections = lax.axis_size("section")
    w_section = weight[0]
    down_matrix = adapter_down_weight[0]
    up_matrix = adapter_up_weight[0]
    below = shifted(sent[1], "section", 1)
    above = shifted(sent[0], "section", -1)
    forward_input = jnp.where(section == 0, embedded, below)
    incoming_gradient = jnp.where(section == sections - 1, loss_gradient, above)
    order = jnp.argsort(table[0])
    arranged = jnp.take(stashed_inputs, order, axis=0)
    fetched = lax.all_to_all(arranged, "section", split_axis=0, concat_axis=0, tiled=True)
    backward_input = fetched.reshape(-1, fetched.shape[-1])
    full_a, full_b = (
        lax.all_gather(forward_input, "tensor", axis=1, tiled=True),
        lax.all_gather(backward_input, "tensor", axis=1, tiled=True),
    )
    main_a = jnp.dot(full_a, w_section, preferred_element_type=jnp.float32)
    h_a = jnp.dot(full_a, down_matrix, preferred_element_type=jnp.float32).astype(jnp.bfloat16)
    u_a = main_a + jnp.dot(h_a, up_matrix, preferred_element_type=jnp.float32)
    value_a, unused = gelu_pair(u_a)
    forward_output = (forward_input.astype(jnp.float32) + value_a).astype(jnp.bfloat16)
    h_b = jnp.dot(full_b, down_matrix, preferred_element_type=jnp.float32).astype(jnp.bfloat16)
    u_b = jnp.dot(full_b, w_section, preferred_element_type=jnp.float32) + jnp.dot(
        h_b, up_matrix, preferred_element_type=jnp.float32
    )
    unused_b, slope_b = gelu_pair(u_b)
    scaled = (incoming_gradient.astype(jnp.float32) * slope_b).astype(jnp.bfloat16)
    low_part = lax.dot_general(
        scaled, up_matrix, (((1,), (1,)), ((), ())), preferred_element_type=jnp.float32
    )
    low_piece = low_part.astype(jnp.bfloat16)
    partial_value = lax.dot_general(
        scaled, w_section, (((1,), (1,)), ((), ())), preferred_element_type=jnp.float32
    )
    partial_value = partial_value + lax.dot_general(
        low_piece, down_matrix, (((1,), (1,)), ((), ())), preferred_element_type=jnp.float32
    )
    input_grad = lax.psum_scatter(
        partial_value.astype(jnp.bfloat16), "tensor", scatter_dimension=1, tiled=True
    ).astype(jnp.float32)
    backward_output = (incoming_gradient.astype(jnp.float32) + input_grad).astype(jnp.bfloat16)
    low_grad = lax.psum(low_part.astype(jnp.bfloat16), "tensor")
    down_term = lax.dot_general(
        backward_input, low_grad, (((0,), (0,)), ((), ())), preferred_element_type=jnp.float32
    )
    up_term = lax.dot_general(
        h_b, scaled, (((0,), (0,)), ((), ())), preferred_element_type=jnp.float32
    )
    down_sum, up_sum = (
        lax.psum(down_term.astype(jnp.bfloat16), "dp").astype(jnp.float32),
        lax.psum(up_term.astype(jnp.bfloat16), "dp").astype(jnp.float32),
    )
    down_gradient = down_sum.astype(jnp.bfloat16)
    up_gradient = up_sum.astype(jnp.bfloat16)
    return (forward_output[None], backward_output[None], down_gradient[None], up_gradient[None])


def solution(mesh):
    placed = (
        P("section", "dp", "tensor"),
        P("section", "dp", "tensor"),
        P("section", None),
        P("dp", "tensor"),
        P("dp", "tensor"),
        P("section", None, "tensor"),
        P("section", None, None),
        P("section", None, "tensor"),
    )
    return jax.shard_map(
        on_device,
        mesh=mesh,
        in_specs=placed,
        out_specs=(
            P("section", "dp", "tensor"),
            P("section", "dp", "tensor"),
            P("section", "tensor", None),
            P("section", None, "tensor"),
        ),
        check_vma=False,
    )
```

profile of v0, /device:TPU:18, one launch (start us, length us, event | category | flops | bytes accessed | tf_op | source)
XLA Modules:
  0.0 162.4 jit_solution(11137440390126994074)
XLA Ops:
  7.2 0.0 copy-start
  7.2 0.0 all-gather.5.cloned.1.call-start
  7.2 1.5 sort.17
  8.8 1.7 %gather_fusion = bf16[4,48,1536]{2,1,0:T(8,128)(2,1)S(1)} fusion(bf16[4,48,1536]{2,1,0:T(8,128)(2,1)} %param.9, s32[1024]{0:T(1024)S(1)} %pad_clamp_fusion), kind=kCustom, calls=%fused_computation | custom fusion | bytes 1179664 | tf_op jit(solution)/shard_map/jit(_take)/gather | solution.py:45
  10.4 0.1 broadcast_select_fusion
  10.6 0.0 copy-start.5
  10.6 18.6 %all_to_all.5 = bf16[4,48,1536]{2,1,0:T(8,128)(2,1)} all-to-all(bf16[4,48,1536]{2,1,0:T(8,128)(2,1)S(1)} %broadcast_select_fusion), channel_id=1, replica_groups=mesh['section'=4,'dp'=2,'tensor'=4] {'section'}, dimensions={0} | all-to-all | bytes 1179648 | tf_op jit(solution)/shard_map/all_to_all | solution.py:46
  29.2 0.0 all-gather.5.cloned.1.call-update
  29.2 0.0 all-gather.3.cloned.1.call-start
  29.2 0.0 copy-done.5
  29.2 1.1 slice_bitcast_fusion
  30.3 3.5 %collective-permute-start = (bf16[192,1536]{1,0:T(8,128)(2,1)}, bf16[192,1536]{1,0:T(8,128)(2,1)S(1)}, u32[]{:S(2)}, u32[]{:S(2)}) collective-permute-start(bf16[192,1536]{1,0:T(8,128)(2,1)} %get-tuple-element.9), channel_id=1, source_target_pairs={{0,8},{8,16},{16,24},{1,9},{9,17},{17,25},{2,10},{10,18},{18,26},{... | collective-permute-start | bytes 1769480 | tf_op jit(solution)/shard_map/ppermute | solution.py:12
  33.9 2.3 %collective-permute-start.1 = (bf16[192,1536]{1,0:T(8,128)(2,1)}, bf16[192,1536]{1,0:T(8,128)(2,1)S(1)}, u32[]{:S(2)}, u32[]{:S(2)}) collective-permute-start(bf16[192,1536]{1,0:T(8,128)(2,1)} %get-tuple-element.8), channel_id=1, source_target_pairs={{8,0},{16,8},{24,16},{9,1},{17,9},{25,17},{10,2},{18,10},{26,18},{... | collective-permute-start | bytes 1769480 | tf_op jit(solution)/shard_map/ppermute | solution.py:12
  36.2 10.7 %collective-permute-done = bf16[192,1536]{1,0:T(8,128)(2,1)S(1)} collective-permute-done((bf16[192,1536]{1,0:T(8,128)(2,1)}, bf16[192,1536]{1,0:T(8,128)(2,1)S(1)}, u32[]{:S(2)}, u32[]{:S(2)}) %collective-permute-start) | collective-permute-done | bytes 589856 | tf_op jit(solution)/shard_map/ppermute | solution.py:12
  46.9 0.9 broadcast_select_fusion.2
  47.8 0.0 all-gather.3.cloned.1.call-update
  47.8 0.0 reduce-scatter.2.cloned.1.call-start
  47.9 6.6 %all-gather.5.cloned.1.call-done = bf16[192,6144]{1,0:T(8,128)(2,1)} async-done(((bf16[192,1536]{1,0:T(8,128)(2,1)}), bf16[192,6144]{1,0:T(8,128)(2,1)}) %all-gather.5.cloned.1.call-update) | async-done | bytes 2359312 | tf_op jit(solution)/shard_map/all_gather | solution.py:50
  54.5 0.0 copy-start.2
  54.5 10.9 %fusion.2 = f32[192,1536]{1,0:T(8,128)S(1)} fusion(bf16[192,6144]{1,0:T(8,128)(2,1)} %all-gather.5.cloned.1.call-done, bf16[1,6144,1536]{2,1,0:T(8,128)(2,1)} %param.13), kind=kOutput, calls=%fused_computation.3 | convolution fusion | flops 3623878656 | bytes 22413312 | tf_op jit(solution)/shard_map/dot_general | solution.py:58
  65.4 0.0 copy-done
  65.5 0.0 copy-done.2
  65.5 0.0 copy-start.4
  65.5 0.0 copy-start.6
  65.5 0.8 fusion.39
  66.3 0.0 collective-permute-done.1
  66.3 0.2 copy-done.4
  66.5 0.2 copy-done.6
  66.7 0.0 copy-start.8
  66.7 1.0 fusion.23
  67.7 0.0 copy-done.8
  67.7 0.3 convolution_convert_fusion.2
  68.0 0.8 fusion.17
  68.8 11.2 %fusion.9 = bf16[192,6144]{1,0:T(8,128)(2,1)} fusion(f32[192,6144]{1,0:T(8,128)S(1)} %fusion.17, bf16[192,1536]{1,0:T(8,128)(2,1)S(1)} %fusion.23, bf16[1,6144,1536]{2,1,0:T(8,128)(2,1)} %param.13), kind=kOutput, calls=%fused_computation.8 | convolution fusion | flops 3626237952 | bytes 26542080 | tf_op jit(solution)/shard_map/dot_general | solution.py:67
  80.0 0.0 reduce-scatter.2.cloned.1.call-update
  80.0 0.0 all-reduce.3.cloned.1.call-start
  80.1 0.6 all-gather.3.cloned.1.call-done
  80.7 3.7 %fusion.43 = f32[192,1536]{1,0:T(8,128)} fusion(bf16[192,6144]{1,0:T(8,128)(2,1)} %all-gather.3.cloned.1.call-done, bf16[1,6144,128]{2,1,0:T(8,128)(2,1)S(1)} %copy-done, bf16[1,128,1536]{2,1,0:T(8,128)(2,1)S(1)} %copy-done.4), kind=kOutput, calls=%fused_computation.42 | convolution fusion | flops 377511936 | bytes 5505024 | tf_op jit(solution)/shard_map/dot_general | solution.py:54
  84.5 0.0 copy-start.1
  84.5 11.0 %psum.21 = bf16[192,128]{1,0:T(8,128)(2,1)S(1)} all-reduce(bf16[192,128]{1,0:T(8,128)(2,1)S(1)} %convolution_convert_fusion.2), channel_id=1, replica_groups=mesh['section'=4,'dp'=2,'tensor'=4] {'tensor'}, use_global_device_ids=true, to_apply=%region_2.3 | all-reduce | flops 24576 | bytes 98304 | tf_op jit(solution)/shard_map/psum | solution.py:77
  95.4 0.0 copy-start.3
  95.5 1.0 fusion.16
  96.5 0.0 copy-done.1
  96.5 1.2 fusion.15
  97.7 0.0 all-reduce.3.cloned.1.call-update
  97.7 0.0 copy-done.3
  97.7 0.0 copy-start.7
  97.7 0.0 copy-start.9
  97.7 12.7 %fusion.46 = bf16[1,192,1536]{2,1,0:T(8,128)(2,1)} fusion(bf16[192,1536]{1,0:T(8,128)(2,1)S(1)} %copy-done.3, f32[192,1536]{1,0:T(8,128)} %fusion.43, bf16[192,6144]{1,0:T(8,128)(2,1)} %all-gather.3.cloned.1.call-done, bf16[1,6144,1536]{2,1,0:T(8,128)(2,1)} %param.13), kind=kOutput, calls=%fused_computation.46 | convolution fusion | flops 3627417600 | bytes 23592960 | tf_op jit(solution)/shard_map/dot_general | solution.py:52
  110.5 5.6 %reduce-scatter.2.cloned.1.call-done = bf16[192,1536]{1,0:T(8,128)(2,1)} async-done(((bf16[192,6144]{1,0:T(8,128)(2,1)}), bf16[192,1536]{1,0:T(8,128)(2,1)}) %reduce-scatter.2.cloned.1.call-update) | async-done | bytes 589840 | tf_op jit(solution)/shard_map/reduce_scatter | solution.py:73
  116.1 0.0 copy-done.7
  116.1 0.0 copy-done.9
  116.1 2.1 %fusion.45 = bf16[1,192,1536]{2,1,0:T(8,128)(2,1)} fusion(bf16[192,1536]{1,0:T(8,128)(2,1)} %reduce-scatter.2.cloned.1.call-done, bf16[192,1536]{1,0:T(8,128)(2,1)S(1)} %copy-done.7, bf16[192,1536]{1,0:T(8,128)(2,1)S(1)} %copy-done.9, pred[]{:T(512)S(6)} %eq.7), kind=kLoop, calls=%fused_computation.43 | loop fusion | flops 1474560 | bytes 2359297 | tf_op jit(solution)/shard_map/broadcast_in_dim | solution.py:90
  118.2 34.2 %all-reduce.3.cloned.1.call-done = (bf16[1,1536,128]{2,1,0:T(8,128)(2,1)}, bf16[1,128,1536]{2,1,0:T(8,128)(2,1)}) async-done(((bf16[1,1536,128]{2,1,0:T(8,128)(2,1)}, bf16[1,128,1536]{2,1,0:T(8,128)(2,1)}), (bf16[1,1536,128]{2,1,0:T(8,128)(2,1)}, bf16[1,128,1536]{2,1,0:T(8,128)(2,1)})) %all-reduce.3.cloned.1.call-update) | async-done | bytes 786448 | tf_op jit(solution)/shard_map/psum | solution.py:85
  152.4 1.8 %copy.14 = bf16[1,1536,128]{2,1,0:T(8,128)(2,1)} copy(bf16[1,1536,128]{2,1,0:T(8,128)(2,1)} %get-tuple-element.12) | data formatting | bytes 786432
  154.1 1.8 %copy.15 = bf16[1,128,1536]{2,1,0:T(8,128)(2,1)} copy(bf16[1,128,1536]{2,1,0:T(8,128)(2,1)} %get-tuple-element.13) | data formatting | bytes 786432
  (4 shorter events, 0.0 us)
Async XLA Ops:
  7.2 58.3 %copy-start = (bf16[1,6144,128]{2,1,0:T(8,128)(2,1)S(1)}, bf16[1,6144,128]{2,1,0:T(8,128)(2,1)}, u32[]{:S(2)}) copy-start(bf16[1,6144,128]{2,1,0:T(8,128)(2,1)} %param.14) | copy-start | bytes 4718596
  7.2 47.3 %all-gather.5.cloned.1.call-start = ((), (), s32[]{:S(2)}) async-start(), calls=%async_computation.3 | async-start | bytes 2949120 | tf_op jit(solution)/shard_map/all_gather | solution.py:50
  10.6 18.7 %copy-start.5 = (bf16[2,192,1536]{2,1,0:T(8,128)(2,1)S(1)}, bf16[2,192,1536]{2,1,0:T(8,128)(2,1)}, u32[]{:S(2)}) copy-start(bf16[2,192,1536]{2,1,0:T(8,128)(2,1)} %param.8) | copy-start | bytes 3538948
  29.2 51.5 %all-gather.3.cloned.1.call-start = ((), (), s32[]{:S(2)}) async-start(), calls=%async_computation.2 | async-start | bytes 2949120 | tf_op jit(solution)/shard_map/all_gather | solution.py:49
  30.3 16.6 %collective-permute-start = (bf16[192,1536]{1,0:T(8,128)(2,1)}, bf16[192,1536]{1,0:T(8,128)(2,1)S(1)}, u32[]{:S(2)}, u32[]{:S(2)}) collective-permute-start(bf16[192,1536]{1,0:T(8,128)(2,1)} %get-tuple-element.9), channel_id=1, source_target_pairs={{0,8},{8,16},{16,24},{1,9},{9,17},{17,25},{2,10},{10,18},{18,26},{... | collective-permute-start | bytes 1769480 | tf_op jit(solution)/shard_map/ppermute | solution.py:12
  33.9 32.4 %collective-permute-start.1 = (bf16[192,1536]{1,0:T(8,128)(2,1)}, bf16[192,1536]{1,0:T(8,128)(2,1)S(1)}, u32[]{:S(2)}, u32[]{:S(2)}) collective-permute-start(bf16[192,1536]{1,0:T(8,128)(2,1)} %get-tuple-element.8), channel_id=1, source_target_pairs={{8,0},{16,8},{24,16},{9,1},{17,9},{25,17},{10,2},{18,10},{26,18},{... | collective-permute-start | bytes 1769480 | tf_op jit(solution)/shard_map/ppermute | solution.py:12
  47.8 68.3 %reduce-scatter.2.cloned.1.call-start = ((), (), s32[]{:S(2)}) async-start(), calls=%async_computation.4 | async-start | bytes 2949120 | tf_op jit(solution)/shard_map/reduce_scatter | solution.py:73
  54.5 11.0 %copy-start.2 = (bf16[192,6144]{1,0:T(8,128)(2,1)S(1)}, bf16[192,6144]{1,0:T(8,128)(2,1)}, u32[]{:S(2)}) copy-start(bf16[192,6144]{1,0:T(8,128)(2,1)} %all-gather.5.cloned.1.call-done) | copy-start | bytes 7077892
  65.5 1.0 copy-start.4
  65.5 1.2 copy-start.6
  66.7 1.1 copy-start.8
  80.0 72.3 %all-reduce.3.cloned.1.call-start = ((), (), s32[]{:S(2)}) async-start(), calls=%async_computation.5 | async-start | bytes 1572864 | tf_op jit(solution)/shard_map/psum | solution.py:85
  84.5 12.1 %copy-start.1 = (bf16[4,48,1536]{2,1,0:T(8,128)(2,1)S(1)}, bf16[4,48,1536]{2,1,0:T(8,128)(2,1)}, u32[]{:S(2)}) copy-start(bf16[4,48,1536]{2,1,0:T(8,128)(2,1)} %all_to_all.5) | copy-start | bytes 1769476
  95.4 2.3 %copy-start.3 = (bf16[192,1536]{1,0:T(8,128)(2,1)S(1)}, bf16[192,1536]{1,0:T(8,128)(2,1)}, u32[]{:S(2)}) copy-start(bf16[192,1536]{1,0:T(8,128)(2,1)} %broadcast_select_fusion.2) | copy-start | bytes 1769476
  97.7 18.4 %copy-start.7 = (bf16[192,1536]{1,0:T(8,128)(2,1)S(1)}, bf16[192,1536]{1,0:T(8,128)(2,1)}, u32[]{:S(2)}) copy-start(bf16[192,1536]{1,0:T(8,128)(2,1)} %param.12) | copy-start | bytes 1769476
  97.7 18.4 %copy-start.9 = (bf16[192,1536]{1,0:T(8,128)(2,1)S(1)}, bf16[192,1536]{1,0:T(8,128)(2,1)}, u32[]{:S(2)}) copy-start(bf16[192,1536]{1,0:T(8,128)(2,1)} %copy-done.8) | copy-start | bytes 1769476
Sparse Core Ops, SparseCore 0:
  29.3 25.1 all-gather.4
  56.6 24.0 all-gather.2
  83.3 32.7 reduce-scatter.1
  118.9 33.4 all-reduce.2
where the time goes:
time: 166 us; the launch traced here: 162 us
  waiting for transfers between devices  57.9 us (35%)
  matrix products  43.7 us (26%)
  blocking collectives  29.6 us (18%)
  between operations  14 us (8%)
  local copies, waits for them, and re-layouts  6.69 us (4%)
  starting transfers between devices  5.99 us (4%)
  other arithmetic  4.61 us (3%)
    psum x1, waiting for transfers between devices, on_device(): lax.psum(down_term.astype(jnp.bfloat16), 'dp').astype(jnp.float32)  34.2 us
    all_to_all x1, blocking collectives, on_device(): lax.all_to_all(arranged, 'section', split_axis=0, concat_axis=0, tiled=True)  18.6 us
    dot_general x1, matrix products, on_device(): main_a = jnp.dot(full_a, w_section, preferred_element_type=jnp.float32)  12.7 us
    dot_general x1, matrix products, on_device(): lax.dot_general(scaled, w_section, (((1,), (1,)), ((), ())), preferred_el...  11.2 us
    psum x1, blocking collectives, on_device(): low_grad = lax.psum(low_part.astype(jnp.bfloat16), 'tensor')  11 us
    dot_general x1, matrix products, on_device(): jnp.dot(full_b, w_section, preferred_element_type=jnp.float32)  10.9 us
    ppermute x2, waiting for transfers between devices, shifted(): return lax.ppermute(block, axis, route)  10.7 us
    all_gather x1, waiting for transfers between devices, on_device(): lax.all_gather(backward_input, 'tensor', axis=1, tiled=True)  6.65 us
  transfers between devices with their start and end apart: 6, of which 5 were waited for; matrix products, arithmetic and copies ran while one was open for 29% of the time, Pallas kernels for 0%

commit v1 on v0

--- a/solution.py
+++ b/solution.py
@@ -1,6 +1,10 @@
+import functools
+
 import jax
 import jax.numpy as jnp
 from jax import lax
+from jax.experimental import pallas as pl
+from jax.experimental.pallas import tpu as pltpu
 from jax.sharding import PartitionSpec as P
 
 coef = 0.7978845608028654
@@ -90,6 +94,397 @@
     return (forward_output[None], backward_output[None], down_gradient[None], up_gradient[None])
 
 
+F32 = jnp.float32
+BF16 = jnp.bfloat16
+MESH = pl.DeviceIdType.MESH
+
+
+def dot_nn(a, b):
+    return lax.dot_general(a, b, (((1,), (0,)), ((), ())), preferred_element_type=F32)
+
+
+def dot_nt(a, b):
+    return lax.dot_general(a, b, (((1,), (1,)), ((), ())), preferred_element_type=F32)
+
+
+def dot_tn(a, b):
+    return lax.dot_general(a, b, (((0,), (0,)), ((), ())), preferred_element_type=F32)
+
+
+def window_kernel(
+    sections, tile,
+    sent, stash, table, embedded, loss, weight, down, up,
+    out_f, out_b, out_d, out_u,
+    w, dn, upv, xa, xb, g, arranged, u, ua, scaled, low, lowr, hb,
+    p_send, q_send, o_send, p_recv, q_recv, o_recv, own,
+    du_send, du_recv, dd_send, dd_recv,
+    w_sem, d_sem, loc_sem, ex_s, ex_r, az_s, az_r, gz_s, gz_r,
+    bx_s, bx_r, ax_s, ax_r, low_s, low_r, p_s, p_r, q_s, q_r, o_s, o_r, dp_s, dp_r,
+):
+    S = sections
+    s = lax.axis_index("section")
+    d = lax.axis_index("dp")
+    t = lax.axis_index("tensor")
+    t1 = t + 1 - 2 * (t % 2)
+    t2 = (t + 2) % 4
+    t3 = (t1 + 2) % 4
+    rel = [t, t1, t2, t3]
+    piece, cols = stash.shape[1], stash.shape[2]
+    rows = S * piece
+    tiles = cols // tile
+
+    def remote(src, dst, ss, rs, **device):
+        return pltpu.make_async_remote_copy(
+            src_ref=src, dst_ref=dst, send_sem=ss, recv_sem=rs,
+            device_id=device, device_id_type=MESH)
+
+    emb_copy = pltpu.make_async_copy(embedded, xa.at[0], loc_sem.at[0])
+    loss_copy = pltpu.make_async_copy(loss, g, loc_sem.at[1])
+    up_copy = pltpu.make_async_copy(up, upv, loc_sem.at[2])
+    w_copies = [pltpu.make_async_copy(weight.at[rel[r]], w.at[r], w_sem.at[r]) for r in range(4)]
+    d_copies = [pltpu.make_async_copy(down.at[rel[r]], dn.at[r], d_sem.at[r]) for r in range(4)]
+
+    barrier = pltpu.get_barrier_semaphore()
+    for j in range(1, S):
+        pl.semaphore_signal(barrier, inc=1, device_id={"section": (s + j) % S}, device_id_type=MESH)
+    for r in range(1, 4):
+        pl.semaphore_signal(barrier, inc=1, device_id={"tensor": rel[r]}, device_id_type=MESH)
+    pl.semaphore_signal(barrier, inc=1, device_id={"dp": 1 - d}, device_id_type=MESH)
+
+    for j in range(S):
+        dest = (s + j) % S
+        k = jnp.int32(0)
+        for i in range(S):
+            k = jnp.where(table[0, i] == dest, i, k)
+        if j == 0:
+            xb[0, s] = stash[k]
+        else:
+            arranged[j] = stash[k]
+    pl.semaphore_wait(barrier, S + 3)
+
+    ex = [None] + [
+        remote(arranged.at[j], xb.at[0, s], ex_s.at[j], ex_r.at[j], section=(s + j) % S)
+        for j in range(1, S)
+    ]
+    for j in EX_ORDER(S):
+        ex[j].start()
+
+    @pl.when(s == 0)
+    def _():
+        emb_copy.start()
+
+    @pl.when(s == S - 1)
+    def _():
+        loss_copy.start()
+
+    for r in range(4):
+        d_copies[r].start()
+        w_copies[r].start()
+    up_copy.start()
+
+    az = [remote(sent.at[1, c], xa.at[0, c], az_s.at[c], az_r.at[c], section=(s + 1) % S) for c in range(S)]
+    gz = remote(sent.at[0], g, gz_s.at[0], gz_r.at[0], section=(s + S - 1) % S)
+
+    @pl.when(s < S - 1)
+    def _():
+        for c in range(S):
+            az[c].start()
+
+    @pl.when(s > 0)
+    def _():
+        gz.start()
+
+    def hops(x, c, sem_s, sem_r, i):
+        return (
+            remote(x.at[0, c], x.at[1, c], sem_s.at[0, i], sem_r.at[0, i], tensor=t1),
+            remote(x.at[0, c], x.at[2, c], sem_s.at[1, i], sem_r.at[1, i], tensor=t2),
+            remote(x.at[2, c], x.at[3, c], sem_s.at[2, i], sem_r.at[2, i], tensor=t1),
+        )
+
+    b_list = [0] + WAIT_ORDER(S)
+    bh = [hops(xb, (s + S - j) % S, bx_s, bx_r, i) for i, j in enumerate(b_list)]
+    ah = [hops(xa, c, ax_s, ax_r, c) for c in range(S)]
+
+    def b_piece(i):
+        j = b_list[i]
+        if j:
+            src = (s + S - j) % S
+            remote(arranged.at[j], xb.at[0, src], ex_s.at[j], ex_r.at[j], section=src).wait_recv()
+        bh[i][1].start()
+        bh[i][0].start()
+
+    def b_pass(i):
+        bh[i][1].wait_recv()
+        bh[i][2].start()
+
+    def a_piece(c):
+        if c == 0:
+            @pl.when(s == 0)
+            def _():
+                emb_copy.wait()
+
+        @pl.when(s > 0)
+        def _():
+            az[c].wait_recv()
+        ah[c][1].start()
+        ah[c][0].start()
+
+    def a_pass(c):
+        ah[c][1].wait_recv()
+        ah[c][2].start()
+
+    def forward(x, r, acc, first):
+        lhs = x.at[r]
+
+        def body(n, carry):
+            at = pl.ds(pl.multiple_of(n * tile, tile), tile)
+            val = dot_nn(lhs[...].reshape(rows, cols), w[r, :, at])
+            if first:
+                acc[n] = val
+            else:
+                acc[n] = acc[n] + val
+            return carry
+        lax.fori_loop(0, tiles, body, 0)
+
+    def low_of(x, r):
+        return dot_nn(x[r].reshape(rows, cols), dn[r])
+
+    for i in range(S):
+        b_piece(i)
+        if i >= 1:
+            b_pass(i - 1)
+
+    d_copies[0].wait()
+    w_copies[0].wait()
+    forward(xb, 0, u, True)
+    h = low_of(xb, 0)
+    b_pass(S - 1)
+    a_piece(0)
+    for i in range(S):
+        bh[i][0].wait_recv()
+    d_copies[1].wait()
+    w_copies[1].wait()
+    forward(xb, 1, u, False)
+    h = h + low_of(xb, 1)
+    a_piece(1)
+    d_copies[2].wait()
+    w_copies[2].wait()
+    forward(xb, 2, u, False)
+    h = h + low_of(xb, 2)
+    for i in range(S):
+        bh[i][2].wait_recv()
+    d_copies[3].wait()
+    w_copies[3].wait()
+    forward(xb, 3, u, False)
+    h = h + low_of(xb, 3)
+    hb[...] = h.astype(BF16)
+    a_pass(0)
+    for c in range(2, S):
+        a_piece(c)
+        a_pass(c - 1)
+    up_copy.wait()
+
+    def slope_body(n, carry):
+        at = pl.ds(pl.multiple_of(n * tile, tile), tile)
+        unused, slope = gelu_pair(u[n] + dot_nn(hb[...], upv[:, at]))
+        u[n] = slope
+        return carry
+    lax.fori_loop(0, tiles, slope_body, 0)
+
+    @pl.when(s == S - 1)
+    def _():
+        loss_copy.wait()
+
+    @pl.when(s < S - 1)
+    def _():
+        gz.wait_recv()
+
+    def scale_body(n, carry):
+        at = pl.ds(pl.multiple_of(n * tile, tile), tile)
+        scaled[:, at] = (g[:, :, at].reshape(rows, tile).astype(F32) * u[n]).astype(BF16)
+        return carry
+    lax.fori_loop(0, tiles, scale_body, 0)
+
+    low[...] = dot_nt(scaled[...], upv[...]).astype(BF16)
+    lows = [None] + [
+        remote(low, lowr.at[r], low_s.at[r], low_r.at[r], tensor=rel[r]) for r in range(1, 4)
+    ]
+    for r in (2, 3, 1):
+        lows[r].start()
+
+    def up_body(n, carry):
+        at = pl.ds(pl.multiple_of(n * tile, tile), tile)
+        du_send[:, at] = dot_tn(hb[...], scaled[:, at]).astype(BF16)
+        return carry
+    lax.fori_loop(0, tiles, up_body, 0)
+    du = remote(du_send, du_recv, dp_s.at[0], dp_r.at[0], dp=1 - d)
+    du.start()
+
+    def partial(r, n):
+        at = pl.ds(pl.multiple_of(n * tile, tile), tile)
+        return dot_nt(scaled[...], w[r, at, :]) + dot_nt(low[...], dn[r, at, :])
+
+    def p_copy(n):
+        return remote(p_send.at[n], p_recv.at[n], p_s.at[n], p_r.at[n], tensor=t1)
+
+    def q_copy(n):
+        return remote(q_send.at[n], q_recv.at[n], q_s.at[n], q_r.at[n], tensor=t2)
+
+    def o_copy(n):
+        return remote(o_send.at[n], o_recv.at[n], o_s.at[n], o_r.at[n], tensor=t1)
+
+    def p_body(n, carry):
+        p_send[n] = partial(3, n).astype(BF16)
+        p_copy(n).start()
+        return carry
+    lax.fori_loop(0, tiles, p_body, 0)
+
+    def q_body(n, carry):
+        mine = partial(2, n)
+        p_copy(n).wait_recv()
+        q_send[n] = (mine + p_recv[n].astype(F32)).astype(BF16)
+        q_copy(n).start()
+        return carry
+    lax.fori_loop(0, tiles, q_body, 0)
+    a_pass(S - 1)
+
+    total = low[...].astype(F32)
+    for r in range(1, 4):
+        lows[r].wait_recv()
+        total = total + lowr[r].astype(F32)
+    lowr[0] = total.astype(BF16)
+    dd_send[...] = dot_tn(xb[0].reshape(rows, cols), lowr[0]).astype(BF16)
+    dd = remote(dd_send, dd_recv, dp_s.at[1], dp_r.at[1], dp=1 - d)
+    dd.start()
+
+    def o_body(n, carry):
+        o_send[n] = partial(1, n).astype(BF16)
+        o_copy(n).start()
+        return carry
+    lax.fori_loop(0, tiles, o_body, 0)
+
+    def own_body(n, carry):
+        own[n] = partial(0, n)
+        return carry
+    lax.fori_loop(0, tiles, own_body, 0)
+
+    forward(xa, 0, ua, True)
+    h = low_of(xa, 0)
+    for c in range(S):
+        ah[c][0].wait_recv()
+    forward(xa, 1, ua, False)
+    h = h + low_of(xa, 1)
+    forward(xa, 2, ua, False)
+    h = h + low_of(xa, 2)
+    for c in range(S):
+        ah[c][2].wait_recv()
+    forward(xa, 3, ua, False)
+    h = h + low_of(xa, 3)
+    ha = h.astype(BF16)
+    hb2 = lowr.at[1]
+    hb2[...] = ha
+
+    def out_body(n, carry):
+        at = pl.ds(pl.multiple_of(n * tile, tile), tile)
+        value, unused = gelu_pair(ua[n] + dot_nn(lowr[1], upv[:, at]))
+        base = xa[0, :, :, at].reshape(rows, tile).astype(F32)
+        out_f[:, at] = (base + value).astype(BF16)
+        return carry
+    lax.fori_loop(0, tiles, out_body, 0)
+
+    du.wait_recv()
+    out_u[...] = (du_send[...].astype(F32) + du_recv[...].astype(F32)).astype(BF16)
+
+    for n in range(tiles):
+        o_copy(n).wait_recv()
+        q_copy(n).wait_recv()
+        at = pl.ds(n * tile, tile)
+        total = own[n] + o_recv[n].astype(F32) + q_recv[n].astype(F32)
+        out_b[:, at] = (g[:, :, at].reshape(rows, tile).astype(F32) + total).astype(BF16)
+
+    dd.wait_recv()
+    out_d[...] = (dd_send[...].astype(F32) + dd_recv[...].astype(F32)).astype(BF16)
+
+    for j in range(1, S):
+        ex[j].wait_send()
+
+    @pl.when(s < S - 1)
+    def _():
+        for c in range(S):
+            az[c].wait_send()
+
+    @pl.when(s > 0)
+    def _():
+        gz.wait_send()
+    for i in range(S):
+        for hop in range(3):
+            bh[i][hop].wait_send()
+            ah[i][hop].wait_send()
+    for r in range(1, 4):
+        lows[r].wait_send()
+    for n in range(tiles):
+        p_copy(n).wait_send()
+        q_copy(n).wait_send()
+        o_copy(n).wait_send()
+    du.wait_send()
+    dd.wait_send()
+
+
+def EX_ORDER(S):
+    return sorted(range(1, S), key=lambda j: (-min(j, S - j), j))
+
+
+def WAIT_ORDER(S):
+    return sorted(range(1, S), key=lambda j: (min(j, S - j), j))
+
+
+def fused_on_device(sent, stash, table, embedded, loss, weight, down, up):
+    S = lax.axis_size("section")
+    piece, cols = stash.shape[1], stash.shape[2]
+    rows, rank = S * piece, up.shape[1]
+    tile = next(k for k in (512, 256, 128) if cols % k == 0)
+    tiles = cols // tile
+    any_space = pl.BlockSpec(memory_space=pl.ANY)
+    vmem = pl.BlockSpec(memory_space=pltpu.VMEM)
+    smem = pl.BlockSpec(memory_space=pltpu.SMEM)
+    V = pltpu.VMEM
+    dma = lambda *shape: pltpu.SemaphoreType.DMA(shape)
+    block = (tiles, rows, tile)
+    outs = pl.pallas_call(
+        functools.partial(window_kernel, S, tile),
+        out_shape=(
+            jax.ShapeDtypeStruct((rows, cols), BF16),
+            jax.ShapeDtypeStruct((rows, cols), BF16),
+            jax.ShapeDtypeStruct((cols, rank), BF16),
+            jax.ShapeDtypeStruct((rank, cols), BF16),
+        ),
+        in_specs=[any_space, vmem, smem, any_space, any_space, any_space, any_space, any_space],
+        out_specs=(vmem,) * 4,
+        scratch_shapes=[
+            V((4, cols, cols), BF16), V((4, cols, rank), BF16), V((rank, cols), BF16),
+            V((4, S, piece, cols), BF16), V((4, S, piece, cols), BF16),
+            V((S, piece, cols), BF16), V((S, piece, cols), BF16),
+            V(block, F32), V(block, F32), V((rows, cols), BF16),
+            V((rows, rank), BF16), V((4, rows, rank), BF16), V((rows, rank), BF16),
+            V(block, BF16), V(block, BF16), V(block, BF16),
+            V(block, BF16), V(block, BF16), V(block, BF16), V(block, F32),
+            V((rank, cols), BF16), V((rank, cols), BF16),
+            V((cols, rank), BF16), V((cols, rank), BF16),
+            dma(4), dma(4), dma(3), dma(S), dma(S), dma(S), dma(S), dma(1), dma(1),
+            dma(3, S), dma(3, S), dma(3, S), dma(3, S), dma(4), dma(4),
+            dma(tiles), dma(tiles), dma(tiles), dma(tiles), dma(tiles), dma(tiles),
+            dma(2), dma(2),
+        ],
+        compiler_params=pltpu.CompilerParams(
+            collective_id=0, has_side_effects=True, vmem_limit_bytes=62 * 1024 * 1024),
+    )(
+        sent.reshape(2, S, piece, cols), stash, table,
+        embedded.reshape(S, piece, cols), loss.reshape(S, piece, cols),
+        weight.reshape(4, cols, cols), down.reshape(4, cols, rank), up[0],
+    )
+    return tuple(o[None] for o in outs)
+
+
 def solution(mesh):
     placed = (
         P("section", "dp", "tensor"),
@@ -101,8 +496,18 @@
         P("section", None, None),
         P("section", None, "tensor"),
     )
-    return jax.shard_map(
-        on_device,
+    def program(*args):
+        rows = args[1].shape[1] // mesh.shape["dp"]
+        cols = args[1].shape[2] // mesh.shape["tensor"]
+        fits = (
+            mesh.shape["tensor"] == 4 and mesh.shape["dp"] == 2
+            and rows % 16 == 0 and cols % 128 == 0
+        )
+        return sharded(fused_on_device if fits else on_device)(*args)
+
+    def sharded(body):
+      return jax.shard_map(
+        body,
         mesh=mesh,
         in_specs=placed,
         out_specs=(
@@ -113,3 +518,5 @@
         ),
         check_vma=False,
     )
+
+    return program

time: 166 us -> 67.6 us (0.41); the launches traced: 162 us -> 67.4 us
  Pallas kernels: 0 us -> 62.4 us
  waiting for transfers between devices: 57.9 us -> 0 us
  matrix products: 43.7 us -> 0 us
  blocking collectives: 29.6 us -> 0 us
  between operations: 14 us -> 0.67 us
  starting transfers between devices: 5.99 us -> 0 us
  other arithmetic: 4.61 us -> 0 us
  local copies, waits for them, and re-layouts: 6.69 us -> 4.34 us
    pallas_call x0 -> x1, Pallas kernels: none -> 62.4 us  [fused_on_device(): pl.pallas_call(functools.partial(window_kernel, S, tile), out_shape=(jax....]
    dot_general x10 -> x0, matrix products: 43.7 us -> none  [the longest x1 12.7 us: on_device(): main_a = jnp.dot(full_a, w_section, preferred_element_type=jnp.float32)]
    psum x1 -> x0, waiting for transfers between devices: 34.2 us -> none  [on_device(): lax.psum(down_term.astype(jnp.bfloat16), 'dp').astype(jnp.float32)]
    all_to_all x1 -> x0, blocking collectives: 18.6 us -> none  [on_device(): lax.all_to_all(arranged, 'section', split_axis=0, concat_axis=0, tiled=True)]
    psum x1 -> x0, blocking collectives: 11 us -> none  [on_device(): low_grad = lax.psum(low_part.astype(jnp.bfloat16), 'tensor')]
    ppermute x2 -> x0, waiting for transfers between devices: 10.7 us -> none  [shifted(): return lax.ppermute(block, axis, route)]
    all_gather x2 -> x0, waiting for transfers between devices: 7.29 us -> none  [the longest x1 6.65 us: on_device(): lax.all_gather(backward_input, 'tensor', axis=1, tiled=True)]
    ppermute x2 -> x0, starting transfers between devices: 5.83 us -> none  [shifted(): return lax.ppermute(block, axis, route)]
  transfers between devices with their start and end apart: 6 -> 0, of which waited for: 5 -> 0; matrix products, arithmetic and copies ran while one was open for 29% -> 0% of each run, Pallas kernels for 0% -> 0%
where the time goes in v1:
time: 67.6 us; the launch traced here: 67.4 us
  Pallas kernels  62.4 us (92%)
  local copies, waits for them, and re-layouts  4.34 us (6%)
    pallas_call x1, Pallas kernels, fused_on_device(): pl.pallas_call(functools.partial(window_kernel, S, tile), out_shape=(jax....  62.4 us
    unnamed x10, local copies, waits for them, and re-layouts  4.34 us

profile of v1, /device:TPU:18, one launch (start us, length us, event | category | flops | bytes accessed | tf_op | source)
XLA Modules:
  0.0 67.4 jit_solution(7054564194612259145)
XLA Ops:
  0.6 62.4 %shard_map.111 = (bf16[192,1536]{1,0:T(8,128)(2,1)}, bf16[192,1536]{1,0:T(8,128)(2,1)}, bf16[1536,128]{1,0:T(8,128)(2,1)}, bf16[128,1536]{1,0:T(8,128)(2,1)}) custom-call(bf16[2,4,48,1536]{3,2,1,0:T(8,128)(2,1)} %bitcast.12, bf16[4,48,1536]{2,1,0:T(8,128)(2,1)} %stash.1, s32[1,4]{1,0:T(1,128)} %table.1, bf16[4,48,1536]{2,1,0:T(8,128)(2,1)} %bitcast.13, ...), custom_call_target="tpu_custom_call" | custom-call | tf_op jit(solution)/shard_map/pallas_call | solution.py:453
  63.1 0.0 copy-start
  63.1 0.0 copy-start.2
  63.1 0.0 copy-start.1
  63.1 2.0 %copy.16 = bf16[1,192,1536]{2,1,0:T(8,128)(2,1)} copy(bf16[1,192,1536]{2,1,0:T(8,128)(2,1)} %bitcast.16) | data formatting | bytes 1179648
  65.1 0.0 copy-done
  65.1 0.8 %copy.17 = bf16[1,192,1536]{2,1,0:T(8,128)(2,1)} copy(bf16[1,192,1536]{2,1,0:T(8,128)(2,1)S(1)} %bitcast.15) | data formatting | bytes 1179648
  65.9 0.0 copy-done.2
  65.9 0.7 %copy.18 = bf16[1,1536,128]{2,1,0:T(8,128)(2,1)} copy(bf16[1,1536,128]{2,1,0:T(8,128)(2,1)S(1)} %bitcast.18) | data formatting | bytes 786432
  66.7 0.0 copy-done.1
  66.7 0.7 %copy.19 = bf16[1,128,1536]{2,1,0:T(8,128)(2,1)} copy(bf16[1,128,1536]{2,1,0:T(8,128)(2,1)S(1)} %bitcast.17) | data formatting | bytes 786432
Async XLA Ops:
  63.1 2.1 %copy-start = (bf16[192,1536]{1,0:T(8,128)(2,1)S(1)}, bf16[192,1536]{1,0:T(8,128)(2,1)}, u32[]{:S(2)}) copy-start(bf16[192,1536]{1,0:T(8,128)(2,1)} %get-tuple-element.9) | copy-start | bytes 1769476
  63.1 2.9 %copy-start.2 = (bf16[1536,128]{1,0:T(8,128)(2,1)S(1)}, bf16[1536,128]{1,0:T(8,128)(2,1)}, u32[]{:S(2)}) copy-start(bf16[1536,128]{1,0:T(8,128)(2,1)} %get-tuple-element.10) | copy-start | bytes 1179652
  63.1 3.6 %copy-start.1 = (bf16[128,1536]{1,0:T(8,128)(2,1)S(1)}, bf16[128,1536]{1,0:T(8,128)(2,1)}, u32[]{:S(2)}) copy-start(bf16[128,1536]{1,0:T(8,128)(2,1)} %get-tuple-element.11) | copy-start | bytes 1179652

commit v2 on v1

--- a/solution.py
+++ b/solution.py
@@ -113,13 +113,13 @@
 
 def window_kernel(
     sections, tile,
-    sent, stash, table, embedded, loss, weight, down, up,
+    sent, stash_hbm, table, embedded, loss, weight, down, up,
     out_f, out_b, out_d, out_u,
-    w, dn, upv, xa, xb, g, arranged, u, ua, scaled, low, lowr, hb,
+    stash_v, w, dn, upv, xa, xb, g, arranged, u, ua, scaled, low, lowr, hb,
     p_send, q_send, o_send, p_recv, q_recv, o_recv, own,
-    du_send, du_recv, dd_send, dd_recv,
+    du_send, du_recv, xo, lg, lg_recv,
     w_sem, d_sem, loc_sem, ex_s, ex_r, az_s, az_r, gz_s, gz_r,
-    bx_s, bx_r, ax_s, ax_r, low_s, low_r, p_s, p_r, q_s, q_r, o_s, o_r, dp_s, dp_r,
+    xo_s, xo_r, bx_s, bx_r, ax_s, ax_r, low_s, low_r, p_s, p_r, q_s, q_r, o_s, o_r, dp_s, dp_r,
 ):
     S = sections
     s = lax.axis_index("section")
@@ -129,16 +129,18 @@
     t2 = (t + 2) % 4
     t3 = (t1 + 2) % 4
     rel = [t, t1, t2, t3]
-    piece, cols = stash.shape[1], stash.shape[2]
+    piece, cols = stash_v.shape[1], stash_v.shape[2]
     rows = S * piece
     tiles = cols // tile
+    stash_copy = pltpu.make_async_copy(stash_hbm, stash_v, loc_sem.at[0])
+    stash_copy.start()
 
     def remote(src, dst, ss, rs, **device):
         return pltpu.make_async_remote_copy(
             src_ref=src, dst_ref=dst, send_sem=ss, recv_sem=rs,
             device_id=device, device_id_type=MESH)
 
-    emb_copy = pltpu.make_async_copy(embedded, xa.at[0], loc_sem.at[0])
+    emb_copy = pltpu.make_async_copy(embedded, xa.at[0], loc_sem.at[3])
     loss_copy = pltpu.make_async_copy(loss, g, loc_sem.at[1])
     up_copy = pltpu.make_async_copy(up, upv, loc_sem.at[2])
     w_copies = [pltpu.make_async_copy(weight.at[rel[r]], w.at[r], w_sem.at[r]) for r in range(4)]
@@ -151,15 +153,16 @@
         pl.semaphore_signal(barrier, inc=1, device_id={"tensor": rel[r]}, device_id_type=MESH)
     pl.semaphore_signal(barrier, inc=1, device_id={"dp": 1 - d}, device_id_type=MESH)
 
+    stash_copy.wait()
     for j in range(S):
         dest = (s + j) % S
         k = jnp.int32(0)
         for i in range(S):
             k = jnp.where(table[0, i] == dest, i, k)
         if j == 0:
-            xb[0, s] = stash[k]
+            xb[0, s] = stash_v[k]
         else:
-            arranged[j] = stash[k]
+            arranged[j] = stash_v[k]
     pl.semaphore_wait(barrier, S + 3)
 
     ex = [None] + [
@@ -204,6 +207,11 @@
     b_list = [0] + WAIT_ORDER(S)
     bh = [hops(xb, (s + S - j) % S, bx_s, bx_r, i) for i, j in enumerate(b_list)]
     ah = [hops(xa, c, ax_s, ax_r, c) for c in range(S)]
+
+    xos = [
+        remote(xb.at[0, (s + S - j) % S], xo.at[(s + S - j) % S], xo_s.at[i], xo_r.at[i], dp=1 - d)
+        for i, j in enumerate(b_list)
+    ]
 
     def b_piece(i):
         j = b_list[i]
@@ -212,6 +220,7 @@
             remote(arranged.at[j], xb.at[0, src], ex_s.at[j], ex_r.at[j], section=src).wait_recv()
         bh[i][1].start()
         bh[i][0].start()
+        xos[i].start()
 
     def b_pass(i):
         bh[i][1].wait_recv()
@@ -278,18 +287,18 @@
     forward(xb, 3, u, False)
     h = h + low_of(xb, 3)
     hb[...] = h.astype(BF16)
+    up_copy.wait()
+
+    def slope_body(n, carry):
+        at = pl.ds(pl.multiple_of(n * tile, tile), tile)
+        unused, slope = gelu_pair(u[n] + dot_nn(hb[...], upv[:, at]))
+        u[n] = slope
+        return carry
+    lax.fori_loop(0, tiles, slope_body, 0)
     a_pass(0)
     for c in range(2, S):
         a_piece(c)
         a_pass(c - 1)
-    up_copy.wait()
-
-    def slope_body(n, carry):
-        at = pl.ds(pl.multiple_of(n * tile, tile), tile)
-        unused, slope = gelu_pair(u[n] + dot_nn(hb[...], upv[:, at]))
-        u[n] = slope
-        return carry
-    lax.fori_loop(0, tiles, slope_body, 0)
 
     @pl.when(s == S - 1)
     def _():
@@ -312,6 +321,25 @@
     for r in (2, 3, 1):
         lows[r].start()
 
+    def partial(r, n):
+        at = pl.ds(pl.multiple_of(n * tile, tile), tile)
+        return dot_nt(scaled[...], w[r, at, :]) + dot_nt(low[...], dn[r, at, :])
+
+    def p_copy(n):
+        return remote(p_send.at[n], p_recv.at[n], p_s.at[n], p_r.at[n], tensor=t1)
+
+    def q_copy(n):
+        return remote(q_send.at[n], q_recv.at[n], q_s.at[n], q_r.at[n], tensor=t2)
+
+    def o_copy(n):
+        return remote(o_send.at[n], o_recv.at[n], o_s.at[n], o_r.at[n], tensor=t1)
+
+    def p_body(n, carry):
+        p_send[n] = partial(3, n).astype(BF16)
+        p_copy(n).start()
+        return carry
+    lax.fori_loop(0, tiles, p_body, 0)
+
     def up_body(n, carry):
         at = pl.ds(pl.multiple_of(n * tile, tile), tile)
         du_send[:, at] = dot_tn(hb[...], scaled[:, at]).astype(BF16)
@@ -319,25 +347,6 @@
     lax.fori_loop(0, tiles, up_body, 0)
     du = remote(du_send, du_recv, dp_s.at[0], dp_r.at[0], dp=1 - d)
     du.start()
-
-    def partial(r, n):
-        at = pl.ds(pl.multiple_of(n * tile, tile), tile)
-        return dot_nt(scaled[...], w[r, at, :]) + dot_nt(low[...], dn[r, at, :])
-
-    def p_copy(n):
-        return remote(p_send.at[n], p_recv.at[n], p_s.at[n], p_r.at[n], tensor=t1)
-
-    def q_copy(n):
-        return remote(q_send.at[n], q_recv.at[n], q_s.at[n], q_r.at[n], tensor=t2)
-
-    def o_copy(n):
-        return remote(o_send.at[n], o_recv.at[n], o_s.at[n], o_r.at[n], tensor=t1)
-
-    def p_body(n, carry):
-        p_send[n] = partial(3, n).astype(BF16)
-        p_copy(n).start()
-        return carry
-    lax.fori_loop(0, tiles, p_body, 0)
 
     def q_body(n, carry):
         mine = partial(2, n)
@@ -352,9 +361,8 @@
     for r in range(1, 4):
         lows[r].wait_recv()
         total = total + lowr[r].astype(F32)
-    lowr[0] = total.astype(BF16)
-    dd_send[...] = dot_tn(xb[0].reshape(rows, cols), lowr[0]).astype(BF16)
-    dd = remote(dd_send, dd_recv, dp_s.at[1], dp_r.at[1], dp=1 - d)
+    lg[...] = total.astype(BF16)
+    dd = remote(lg, lg_recv, dp_s.at[1], dp_r.at[1], dp=1 - d)
     dd.start()
 
     def o_body(n, carry):
@@ -395,6 +403,13 @@
     du.wait_recv()
     out_u[...] = (du_send[...].astype(F32) + du_recv[...].astype(F32)).astype(BF16)
 
+    for i in range(S):
+        xos[i].wait_recv()
+    dd.wait_recv()
+    here = dot_tn(xb[0].reshape(rows, cols), lg[...]).astype(BF16)
+    there = dot_tn(xo[...].reshape(rows, cols), lg_recv[...]).astype(BF16)
+    out_d[...] = (here.astype(F32) + there.astype(F32)).astype(BF16)
+
     for n in range(tiles):
         o_copy(n).wait_recv()
         q_copy(n).wait_recv()
@@ -402,9 +417,6 @@
         total = own[n] + o_recv[n].astype(F32) + q_recv[n].astype(F32)
         out_b[:, at] = (g[:, :, at].reshape(rows, tile).astype(F32) + total).astype(BF16)
 
-    dd.wait_recv()
-    out_d[...] = (dd_send[...].astype(F32) + dd_recv[...].astype(F32)).astype(BF16)
-
     for j in range(1, S):
         ex[j].wait_send()
 
@@ -417,6 +429,7 @@
     def _():
         gz.wait_send()
     for i in range(S):
+        xos[i].wait_send()
         for hop in range(3):
             bh[i][hop].wait_send()
             ah[i][hop].wait_send()
@@ -430,6 +443,17 @@
     dd.wait_send()
 
 
+def finish_kernel(*refs):
+    sems, count = refs[-1], (len(refs) - 1) // 2
+    copies = [
+        pltpu.make_async_copy(refs[i], refs[count + i], sems.at[i]) for i in range(count)
+    ]
+    for copy in copies:
+        copy.start()
+    for copy in copies:
+        copy.wait()
+
+
 def EX_ORDER(S):
     return sorted(range(1, S), key=lambda j: (-min(j, S - j), j))
 
@@ -445,6 +469,7 @@
     tile = next(k for k in (512, 256, 128) if cols % k == 0)
     tiles = cols // tile
     any_space = pl.BlockSpec(memory_space=pl.ANY)
+    hbm = pl.BlockSpec(memory_space=pltpu.HBM)
     vmem = pl.BlockSpec(memory_space=pltpu.VMEM)
     smem = pl.BlockSpec(memory_space=pltpu.SMEM)
     V = pltpu.VMEM
@@ -458,10 +483,10 @@
             jax.ShapeDtypeStruct((cols, rank), BF16),
             jax.ShapeDtypeStruct((rank, cols), BF16),
         ),
-        in_specs=[any_space, vmem, smem, any_space, any_space, any_space, any_space, any_space],
+        in_specs=[hbm, hbm, smem, hbm, hbm, hbm, hbm, hbm],
         out_specs=(vmem,) * 4,
         scratch_shapes=[
-            V((4, cols, cols), BF16), V((4, cols, rank), BF16), V((rank, cols), BF16),
+            V((S, piece, cols), BF16), V((4, cols, cols), BF16), V((4, cols, rank), BF16), V((rank, cols), BF16),
             V((4, S, piece, cols), BF16), V((4, S, piece, cols), BF16),
             V((S, piece, cols), BF16), V((S, piece, cols), BF16),
             V(block, F32), V(block, F32), V((rows, cols), BF16),
@@ -469,19 +494,27 @@
             V(block, BF16), V(block, BF16), V(block, BF16),
             V(block, BF16), V(block, BF16), V(block, BF16), V(block, F32),
             V((rank, cols), BF16), V((rank, cols), BF16),
-            V((cols, rank), BF16), V((cols, rank), BF16),
-            dma(4), dma(4), dma(3), dma(S), dma(S), dma(S), dma(S), dma(1), dma(1),
+            V((S, piece, cols), BF16), V((rows, rank), BF16), V((rows, rank), BF16),
+            dma(4), dma(4), dma(4), dma(S), dma(S), dma(S), dma(S), dma(1), dma(1), dma(S), dma(S),
             dma(3, S), dma(3, S), dma(3, S), dma(3, S), dma(4), dma(4),
             dma(tiles), dma(tiles), dma(tiles), dma(tiles), dma(tiles), dma(tiles),
             dma(2), dma(2),
         ],
         compiler_params=pltpu.CompilerParams(
-            collective_id=0, has_side_effects=True, vmem_limit_bytes=62 * 1024 * 1024),
+            collective_id=0, has_side_effects=True, vmem_limit_bytes=60 * 1024 * 1024),
     )(
         sent.reshape(2, S, piece, cols), stash, table,
         embedded.reshape(S, piece, cols), loss.reshape(S, piece, cols),
         weight.reshape(4, cols, cols), down.reshape(4, cols, rank), up[0],
     )
+    outs = pl.pallas_call(
+        finish_kernel,
+        out_shape=tuple(jax.ShapeDtypeStruct(o.shape, o.dtype) for o in outs),
+        in_specs=(vmem,) * 4,
+        out_specs=(any_space,) * 4,
+        scratch_shapes=[dma(4)],
+        compiler_params=pltpu.CompilerParams(vmem_limit_bytes=8 * 1024 * 1024),
+    )(*outs)
     return tuple(o[None] for o in outs)
 
 

time: 67.6 us -> 68.3 us (1.010)
  Pallas kernels: 62.4 us -> 63.2 us
    pallas_call x0 -> x1, Pallas kernels: none -> 1.3 us  [fused_on_device(): pl.pallas_call(finish_kernel, out_shape=tuple((jax.ShapeDtypeStruct(o.sha...]
    unnamed x10 -> x8, local copies, waits for them, and re-layouts: 4.34 us -> 4.11 us
where the time goes in v2:
time: 68.3 us; the launch traced here: 68 us
  Pallas kernels  63.2 us (93%)
  local copies, waits for them, and re-layouts  4.11 us (6%)
    pallas_call x1, Pallas kernels, fused_on_device(): pl.pallas_call(functools.partial(window_kernel, S, tile), out_shape=(jax....  61.9 us
    unnamed x8, local copies, waits for them, and re-layouts  4.11 us

profile of v2, /device:TPU:18, one launch (start us, length us, event | category | flops | bytes accessed | tf_op | source)
XLA Modules:
  0.0 68.0 jit_solution(6362133456932746097)
XLA Ops:
  0.6 61.9 %shard_map.111 = (bf16[192,1536]{1,0:T(8,128)(2,1)}, bf16[192,1536]{1,0:T(8,128)(2,1)}, bf16[1536,128]{1,0:T(8,128)(2,1)}, bf16[128,1536]{1,0:T(8,128)(2,1)}) custom-call(bf16[2,4,48,1536]{3,2,1,0:T(8,128)(2,1)} %bitcast.12, bf16[4,48,1536]{2,1,0:T(8,128)(2,1)} %stash_hbm.1, s32[1,4]{1,0:T(1,128)} %table.1, bf16[4,48,1536]{2,1,0:T(8,128)(2,1)} %bitcast.13, ...), custom_call_target="tpu_custom_call" | custom-call | tf_op jit(solution)/shard_map/pallas_call | solution.py:478
  62.5 0.0 copy-start
  62.6 1.1 %copy-done = bf16[192,1536]{1,0:T(8,128)(2,1)S(1)} copy-done((bf16[192,1536]{1,0:T(8,128)(2,1)S(1)}, bf16[192,1536]{1,0:T(8,128)(2,1)}, u32[]{:S(2)}) %copy-start) | copy-done | bytes 589848
  63.6 0.0 copy-start.1
  63.6 1.1 %copy-done.1 = bf16[192,1536]{1,0:T(8,128)(2,1)S(1)} copy-done((bf16[192,1536]{1,0:T(8,128)(2,1)S(1)}, bf16[192,1536]{1,0:T(8,128)(2,1)}, u32[]{:S(2)}) %copy-start.1) | copy-done | bytes 589848
  64.7 0.0 copy-start.2
  64.7 1.0 %copy-done.2 = bf16[1536,128]{1,0:T(8,128)(2,1)S(1)} copy-done((bf16[1536,128]{1,0:T(8,128)(2,1)S(1)}, bf16[1536,128]{1,0:T(8,128)(2,1)}, u32[]{:S(2)}) %copy-start.2) | copy-done | bytes 393240
  65.7 0.0 copy-start.3
  65.7 1.0 %copy-done.3 = bf16[128,1536]{1,0:T(8,128)(2,1)S(1)} copy-done((bf16[128,1536]{1,0:T(8,128)(2,1)S(1)}, bf16[128,1536]{1,0:T(8,128)(2,1)}, u32[]{:S(2)}) %copy-start.3) | copy-done | bytes 393240
  66.7 1.3 %shard_map.112 = (bf16[192,1536]{1,0:T(8,128)(2,1)}, bf16[192,1536]{1,0:T(8,128)(2,1)}, bf16[1536,128]{1,0:T(8,128)(2,1)}, bf16[128,1536]{1,0:T(8,128)(2,1)}) custom-call(bf16[192,1536]{1,0:T(8,128)(2,1)S(1)} %copy-done, bf16[192,1536]{1,0:T(8,128)(2,1)S(1)} %copy-done.1, bf16[1536,128]{1,0:T(8,128)(2,1)S(1)} %copy-done.2, bf16[128,1536]{1,0:T(8,128)(2,1)S(1)} %copy-done.3), custom_call_target="tpu_custom_call" | custom-call | tf_op jit(solution)/shard_map/pallas_call | solution.py:510
Async XLA Ops:
  62.5 1.1 %copy-start = (bf16[192,1536]{1,0:T(8,128)(2,1)S(1)}, bf16[192,1536]{1,0:T(8,128)(2,1)}, u32[]{:S(2)}) copy-start(bf16[192,1536]{1,0:T(8,128)(2,1)} %get-tuple-element.12.refs_0_) | copy-start | bytes 1769476
  63.6 1.1 %copy-start.1 = (bf16[192,1536]{1,0:T(8,128)(2,1)S(1)}, bf16[192,1536]{1,0:T(8,128)(2,1)}, u32[]{:S(2)}) copy-start(bf16[192,1536]{1,0:T(8,128)(2,1)} %get-tuple-element.13.refs_1_) | copy-start | bytes 1769476
  64.7 1.0 %copy-start.2 = (bf16[1536,128]{1,0:T(8,128)(2,1)S(1)}, bf16[1536,128]{1,0:T(8,128)(2,1)}, u32[]{:S(2)}) copy-start(bf16[1536,128]{1,0:T(8,128)(2,1)} %get-tuple-element.14.refs_2_) | copy-start | bytes 1179652
  65.7 1.0 %copy-start.3 = (bf16[128,1536]{1,0:T(8,128)(2,1)S(1)}, bf16[128,1536]{1,0:T(8,128)(2,1)}, u32[]{:S(2)}) copy-start(bf16[128,1536]{1,0:T(8,128)(2,1)} %get-tuple-element.15.refs_3_) | copy-start | bytes 1179652

commit v3 on v2

--- a/solution.py
+++ b/solution.py
@@ -443,17 +443,6 @@
     dd.wait_send()
 
 
-def finish_kernel(*refs):
-    sems, count = refs[-1], (len(refs) - 1) // 2
-    copies = [
-        pltpu.make_async_copy(refs[i], refs[count + i], sems.at[i]) for i in range(count)
-    ]
-    for copy in copies:
-        copy.start()
-    for copy in copies:
-        copy.wait()
-
-
 def EX_ORDER(S):
     return sorted(range(1, S), key=lambda j: (-min(j, S - j), j))
 
@@ -466,7 +455,7 @@
     S = lax.axis_size("section")
     piece, cols = stash.shape[1], stash.shape[2]
     rows, rank = S * piece, up.shape[1]
-    tile = next(k for k in (512, 256, 128) if cols % k == 0)
+    tile = next(k for k in (768, 512, 256, 128) if cols % k == 0)
     tiles = cols // tile
     any_space = pl.BlockSpec(memory_space=pl.ANY)
     hbm = pl.BlockSpec(memory_space=pltpu.HBM)
@@ -507,14 +496,6 @@
         embedded.reshape(S, piece, cols), loss.reshape(S, piece, cols),
         weight.reshape(4, cols, cols), down.reshape(4, cols, rank), up[0],
     )
-    outs = pl.pallas_call(
-        finish_kernel,
-        out_shape=tuple(jax.ShapeDtypeStruct(o.shape, o.dtype) for o in outs),
-        in_specs=(vmem,) * 4,
-        out_specs=(any_space,) * 4,
-        scratch_shapes=[dma(4)],
-        compiler_params=pltpu.CompilerParams(vmem_limit_bytes=8 * 1024 * 1024),
-    )(*outs)
     return tuple(o[None] for o in outs)
 
 

time: 68.3 us -> 65.5 us (0.959)
  Pallas kernels: 63.2 us -> 60.2 us
    pallas_call x1, Pallas kernels: 61.9 us -> 60.2 us  [fused_on_device(): pl.pallas_call(functools.partial(window_kernel, S, tile), out_shape=(jax....]
    pallas_call x1 -> x0, Pallas kernels: 1.3 us -> none  [fused_on_device(): pl.pallas_call(finish_kernel, out_shape=tuple((jax.ShapeDtypeStruct(o.sha...]
    unnamed x8 -> x10, local copies, waits for them, and re-layouts: 4.11 us -> 4.34 us
where the time goes in v3:
time: 65.5 us; the launch traced here: 65.2 us
  Pallas kernels  60.2 us (92%)
  local copies, waits for them, and re-layouts  4.34 us (7%)
  between operations  0.67 us (1%)
    pallas_call x1, Pallas kernels, fused_on_device(): pl.pallas_call(functools.partial(window_kernel, S, tile), out_shape=(jax....  60.2 us
    unnamed x10, local copies, waits for them, and re-layouts  4.34 us

profile of v3, /device:TPU:18, one launch (start us, length us, event | category | flops | bytes accessed | tf_op | source)
XLA Modules:
  0.0 65.2 jit_solution(1003119364642946558)
XLA Ops:
  0.6 60.2 %shard_map.111 = (bf16[192,1536]{1,0:T(8,128)(2,1)}, bf16[192,1536]{1,0:T(8,128)(2,1)}, bf16[1536,128]{1,0:T(8,128)(2,1)}, bf16[128,1536]{1,0:T(8,128)(2,1)}) custom-call(bf16[2,4,48,1536]{3,2,1,0:T(8,128)(2,1)} %bitcast.12, bf16[4,48,1536]{2,1,0:T(8,128)(2,1)} %stash_hbm.1, s32[1,4]{1,0:T(1,128)} %table.1, bf16[4,48,1536]{2,1,0:T(8,128)(2,1)} %bitcast.13, ...), custom_call_target="tpu_custom_call" | custom-call | tf_op jit(solution)/shard_map/pallas_call | solution.py:467
  60.8 0.0 copy-start
  60.8 0.0 copy-start.2
  60.8 0.0 copy-start.1
  60.8 2.0 %copy.16 = bf16[1,192,1536]{2,1,0:T(8,128)(2,1)} copy(bf16[1,192,1536]{2,1,0:T(8,128)(2,1)} %bitcast.16) | data formatting | bytes 1179648
  62.9 0.0 copy-done
  62.9 0.8 %copy.17 = bf16[1,192,1536]{2,1,0:T(8,128)(2,1)} copy(bf16[1,192,1536]{2,1,0:T(8,128)(2,1)S(1)} %bitcast.15) | data formatting | bytes 1179648
  63.7 0.0 copy-done.2
  63.7 0.7 %copy.18 = bf16[1,1536,128]{2,1,0:T(8,128)(2,1)} copy(bf16[1,1536,128]{2,1,0:T(8,128)(2,1)S(1)} %bitcast.18) | data formatting | bytes 786432
  64.4 0.0 copy-done.1
  64.4 0.7 %copy.19 = bf16[1,128,1536]{2,1,0:T(8,128)(2,1)} copy(bf16[1,128,1536]{2,1,0:T(8,128)(2,1)S(1)} %bitcast.17) | data formatting | bytes 786432
Async XLA Ops:
  60.8 2.1 %copy-start = (bf16[192,1536]{1,0:T(8,128)(2,1)S(1)}, bf16[192,1536]{1,0:T(8,128)(2,1)}, u32[]{:S(2)}) copy-start(bf16[192,1536]{1,0:T(8,128)(2,1)} %get-tuple-element.9) | copy-start | bytes 1769476
  60.8 2.9 %copy-start.2 = (bf16[1536,128]{1,0:T(8,128)(2,1)S(1)}, bf16[1536,128]{1,0:T(8,128)(2,1)}, u32[]{:S(2)}) copy-start(bf16[1536,128]{1,0:T(8,128)(2,1)} %get-tuple-element.10) | copy-start | bytes 1179652
  60.8 3.6 %copy-start.1 = (bf16[128,1536]{1,0:T(8,128)(2,1)S(1)}, bf16[128,1536]{1,0:T(8,128)(2,1)}, u32[]{:S(2)}) copy-start(bf16[128,1536]{1,0:T(8,128)(2,1)} %get-tuple-element.11) | copy-start | bytes 1179652
